TPU v7x, 128 devices: a whole 4x4x4 slice. The times are simulated.
128 devices in a mesh: op: 16 (over x, y), sec: 8 (over z, core).
Axes of the slice: x: 4, y: 4, z: 4, core: 2. Of those that a mesh axis runs over, the one named last changes fastest.
Arguments:
- wave: bfloat16 [32, 256, 4, 256], P('op'), may hold values from -6 to 6
- sector_dims: int32 [32], replicated, may hold values from 64 to 256, as said below
- left_ops: bfloat16 [32, 128, 256, 256], P(None, ('op', 'sec')), may hold values from -0.375 to 0.375
- right_ops: bfloat16 [32, 16, 8, 256, 256], P('op', None, 'sec'), may hold values from -0.375 to 0.375
- site_ops: float32 [128, 4, 4], replicated, may hold values from -0.25 to 0.25
Outputs:
- sigma: bfloat16 [32, 256, 4, 256], P('op', 'sec')
Inputs may be any that keep to these rules, and one draw needn't show every extreme that they name: `sector_dims`: every entry is a multiple of 64, and at least one sector has exactly 256 states.
All inputs are finite; a program needn't handle non-finite values.
Results may differ from a plain program's by a relative error of at most 0.005.
Values may be sent and summed in bfloat16 or wider, within the bound.
No kernel may reach another device: no remote copies, remote signals or barrier semaphores. Data moves between devices by JAX's collectives and lax.ppermute only.
A program may use at most 128 MiB of HBM per device.

v0:
```python
import jax
import jax.numpy as jnp
from jax import lax
from jax.sharding import PartitionSpec as P


def sector_mask(sizes, width):
    places = lax.broadcasted_iota(jnp.int32, (sizes.shape[0], width), 1)
    return (places < sizes[:, None]).astype(jnp.float32)


def left_step(blocks, waves, site_mats):

    def one_sector(inputs):
        ops_block, wave_block = inputs
        first = jnp.einsum(
            "klm,mpr->klpr", ops_block, wave_block, preferred_element_type=jnp.float32
        )
        second = jnp.einsum("klpr,kqp->klqr", first, site_mats, precision=lax.Precision.HIGHEST)
        return second.astype(jnp.bfloat16)

    return lax.map(one_sector, (blocks, waves))


def shards(wave, sector_dims, left_ops, right_ops, site_ops):
    sec_count = lax.axis_size("sec")
    op_index = lax.axis_index("op")
    sec_index = lax.axis_index("sec")
    local_sectors = wave.shape[0]
    width = wave.shape[1]
    term_count = left_ops.shape[1]
    own_sizes = lax.dynamic_slice_in_dim(sector_dims, op_index * local_sectors, local_sectors)
    own_mask = sector_mask(own_sizes, width)
    masked = (
        wave.astype(jnp.float32) * own_mask[:, :, None, None] * own_mask[:, None, None, :]
    ).astype(jnp.bfloat16)
    first_term = (op_index * sec_count + sec_index) * term_count
    site_local = lax.dynamic_slice_in_dim(site_ops, first_term, term_count)
    inter = left_step(left_ops, lax.all_gather(masked, "op", axis=0, tiled=True), site_local)
    inter = lax.all_to_all(inter, "op", split_axis=0, concat_axis=1, tiled=True)
    right_local = right_ops.reshape(local_sectors, -1, width, width)
    partial_sum = jnp.einsum(
        "sklqm,skrm->slqr", inter, right_local, preferred_element_type=jnp.float32
    )
    row_count = width // sec_count
    summed = lax.psum(partial_sum, "sec")
    share = lax.dynamic_slice_in_dim(summed, sec_index * row_count, row_count, 1)
    row_mask = lax.dynamic_slice_in_dim(own_mask, sec_index * row_count, row_count, 1)
    return (share * row_mask[:, :, None, None] * own_mask[:, None, None, :]).astype(jnp.bfloat16)


def solution(mesh):
    placed = (
        P("op", None, None, None),
        P(),
        P(None, ("op", "sec"), None, None),
        P("op", None, "sec", None, None),
        P(),
    )
    return jax.shard_map(
        shards, mesh=mesh, in_specs=placed, out_specs=P("op", "sec", None, None), check_vma=False
    )
```

profile of v0, /device:TPU:0, one launch (start us, length us, event | category | flops | bytes accessed | tf_op | source)
XLA Modules:
  0.0 555.1 jit_solution(4734230497809991994)
XLA Ops:
  7.4 2.5 multiply_convert_fusion
  10.2 113.6 %all-gather.2.cloned.1.call-done = bf16[32,256,4,256]{3,1,2,0:T(8,128)(2,1)} async-done(((bf16[2,256,4,256]{3,1,2,0:T(8,128)(2,1)}), bf16[32,256,4,256]{3,1,2,0:T(8,128)(2,1)}) %all-gather.2.cloned.1.call-update) | async-done | bytes 16777232 | tf_op jit(solution)/shard_map/all_gather | solution.py:39
  123.7 153.4 %while.10 = (s32[]{:T(128)}, bf16[32,1,256,4,256]{4,2,3,1,0:T(8,128)(2,1)}, bf16[32,1,256,256]{3,2,1,0:T(8,128)(2,1)}, bf16[32,256,4,256]{3,1,2,0:T(8,128)(2,1)}, f32[1,4,4]{2,1,0:T(4,128)S(1)}, /*index=5*/s32[]{:T(128)}) while((s32[]{:T(128)}, bf16[32,1,256,4,256]{4,2,3,1,0:T(8,128)(2,1)}, bf16[32,1,256,256]{3,2,1,0:T(8,128)(2,1)}, ...), condition=%wide.region_1.2_spmd, body=%wide.region_0.1_spmd.sunk | while | flops 147062784 | bytes 4327045 | solution.py:22
  123.7 1.4 fusion.23
  125.1 2.5 fusion.24
  129.9 2.5 fusion.24
  134.7 2.5 fusion.24
  139.5 2.5 fusion.24
  144.3 2.5 fusion.24
  149.1 2.5 fusion.24
  153.9 2.5 fusion.24
  158.6 2.5 fusion.24
  162.0 1.4 fusion.23
  163.4 2.5 fusion.24
  166.8 1.4 fusion.23
  168.2 2.5 fusion.24
  171.6 1.4 fusion.23
  173.0 2.5 fusion.24
  176.4 1.4 fusion.23
  177.8 2.5 fusion.24
  182.6 2.5 fusion.24
  187.4 2.5 fusion.24
  192.2 2.5 fusion.24
  196.9 2.5 fusion.24
  201.8 2.5 fusion.24
  206.6 2.5 fusion.24
  211.4 2.5 fusion.24
  216.2 2.5 fusion.24
  219.6 1.4 fusion.23
  221.0 2.5 fusion.24
  225.8 2.5 fusion.24
  230.6 2.5 fusion.24
  233.9 1.4 fusion.23
  235.3 2.5 fusion.24
  240.1 2.5 fusion.24
  243.5 1.4 fusion.23
  245.0 2.5 fusion.24
  249.8 2.5 fusion.24
  254.5 2.5 fusion.24
  257.9 1.4 fusion.23
  259.3 2.5 fusion.24
  264.1 2.5 fusion.24
  268.9 2.5 fusion.24
  273.7 2.5 fusion.24
  277.1 191.8 %all_to_all.18 = bf16[32,1,256,4,256]{4,2,3,1,0:T(8,128)(2,1)} all-to-all(bf16[32,1,256,4,256]{4,2,3,1,0:T(8,128)(2,1)} %get-tuple-element.32), channel_id=1, replica_groups=mesh['op'=16,'sec'=8] {'op'}, dimensions={0} | all-to-all | bytes 33554432 | tf_op jit(solution)/shard_map/all_to_all | solution.py:40
  468.9 9.4 %fusion.9 = f32[2,256,4,256,1]{3,1,2,0,4:T(8,128)S(1)} fusion(bf16[2,16,256,4,256]{4,2,3,0,1:T(8,128)(2,1)} %bitcast.43, bf16[2,16,1,256,256]{4,3,2,1,0:T(8,128)(2,1)} %param.10), kind=kOutput, calls=%fused_computation.11 | convolution fusion | flops 4294967296 | bytes 23068672 | tf_op jit(solution)/shard_map/sklqm,skrm->slqr/dot_general | solution.py:42
  478.3 1.5 copy.35
  479.9 66.6 %all-reduce.2.cloned.1.call-done = f32[2,256,4,256]{3,1,0,2:T(8,128)} async-done(((f32[2,256,4,256]{3,1,0,2:T(8,128)}), f32[2,256,4,256]{3,1,0,2:T(8,128)}) %all-reduce.2.cloned.1.call-update) | async-done | bytes 2097168 | tf_op jit(solution)/shard_map/psum | solution.py:46
  (71 shorter events, 63.6 us)
Async XLA Ops:
  6.5 3.4 copy-start
  6.5 117.2 %all-gather.2.cloned.1.call-start = ((), (), s32[]{:S(2)}) async-start(), calls=%async_computation.1 | async-start | bytes 17825792 | tf_op jit(solution)/shard_map/all_gather | solution.py:39
  9.9 536.6 %all-reduce.2.cloned.1.call-start = ((), (), s32[]{:S(2)}) async-start(), calls=%async_computation.2 | async-start | bytes 4194304 | tf_op jit(solution)/shard_map/psum | solution.py:46
  468.9 79.4 %copy-start.1 = (f32[128,4,4]{0,2,1:T(4,128)S(1)}, f32[128,4,4]{0,2,1:T(4,128)}, u32[]{:S(2)}) copy-start(f32[128,4,4]{0,2,1:T(4,128)} %param.11) | copy-start | bytes 24580
Sparse Core Ops, SparseCore 0:
  10.0 113.6 all-gather.1
  480.0 66.4 all-reduce.1
where the time goes:
time: 556 us; the launch traced here: 555 us
  blocking collectives  192 us (35%)
  waiting for transfers between devices  180 us (32%)
  matrix products  134 us (24%)
  local copies, waits for them, and re-layouts  31.5 us (6%)
  between operations  13.4 us (2%)
    all_to_all x1, blocking collectives, shards(): inter = lax.all_to_all(inter, 'op', split_axis=0, concat_axis=1, tiled=True)  192 us
    all_gather x1, waiting for transfers between devices, shards(): lax.all_gather(masked, 'op', axis=0, tiled=True)  114 us
    dot_general x32, matrix products, one_sector(): jnp.einsum('klpr,kqp->klqr', first, site_mats, precision=lax.Precision.HI...  79.6 us
    psum x1, waiting for transfers between devices, shards(): summed = lax.psum(partial_sum, 'sec')  66.6 us
    dot_general x32, matrix products, one_sector(): jnp.einsum('klm,mpr->klpr', ops_block, wave_block, preferred_element_type...  45.2 us
    dynamic_update_slice x32, local copies, waits for them, and re-layouts, left_step(): return lax.map(one_sector, (blocks, waves))  28.2 us
  transfers between devices with their start and end apart: 2, of which 2 were waited for; matrix products, arithmetic and copies ran while one was open for 0% of the time, Pallas kernels for 0%

commit v1 on v0

--- a/solution.py
+++ b/solution.py
@@ -2,6 +2,14 @@
 import jax.numpy as jnp
 from jax import lax
 from jax.sharding import PartitionSpec as P
+
+
+def tiled_gather(value, axis, dim):
+    devices = lax.axis_size(axis)
+    repeats = [devices if d == dim else 1 for d in range(value.ndim)]
+    return lax.all_to_all(
+        jnp.tile(value, repeats), axis, split_axis=dim, concat_axis=dim, tiled=True
+    )
 
 
 def sector_mask(sizes, width):
@@ -36,7 +44,7 @@
     ).astype(jnp.bfloat16)
     first_term = (op_index * sec_count + sec_index) * term_count
     site_local = lax.dynamic_slice_in_dim(site_ops, first_term, term_count)
-    inter = left_step(left_ops, lax.all_gather(masked, "op", axis=0, tiled=True), site_local)
+    inter = left_step(left_ops, tiled_gather(masked, "op", 0), site_local)
     inter = lax.all_to_all(inter, "op", split_axis=0, concat_axis=1, tiled=True)
     right_local = right_ops.reshape(local_sectors, -1, width, width)
     partial_sum = jnp.einsum(

time: 556 us -> 792 us (1.42)
  waiting for transfers between devices: 180 us -> 363 us
  local copies, waits for them, and re-layouts: 31.5 us -> 76.9 us
    all_to_all x0 -> x1, waiting for transfers between devices: none -> 293 us  [tiled_gather(): lax.all_to_all(jnp.tile(value, repeats), axis, split_axis=dim, concat_axi...]
    all_gather x1 -> x0, waiting for transfers between devices: 114 us -> none  [shards(): lax.all_gather(masked, 'op', axis=0, tiled=True)]
    squeeze x0 -> x32, local copies, waits for them, and re-layouts: none -> 39.1 us  [left_step(): return lax.map(one_sector, (blocks, waves))]
where the time goes in v1:
time: 792 us; the launch traced here: 790 us
  waiting for transfers between devices  363 us (46%)
  blocking collectives  198 us (25%)
  matrix products  128 us (16%)
  local copies, waits for them, and re-layouts  76.9 us (10%)
  between operations  13.5 us (2%)
    all_to_all x1, waiting for transfers between devices, tiled_gather(): lax.all_to_all(jnp.tile(value, repeats), axis, split_axis=dim, concat_axi...  293 us
    all_to_all x1, blocking collectives, shards(): inter = lax.all_to_all(inter, 'op', split_axis=0, concat_axis=1, tiled=True)  198 us
    dot_general x32, matrix products, one_sector(): jnp.einsum('klpr,kqp->klqr', first, site_mats, precision=lax.Precision.HI...  79.6 us
    psum x1, waiting for transfers between devices, shards(): summed = lax.psum(partial_sum, 'sec')  70.5 us
    squeeze x32, local copies, waits for them, and re-layouts, left_step(): return lax.map(one_sector, (blocks, waves))  39.1 us
    dot_general x32, matrix products, one_sector(): jnp.einsum('klm,mpr->klpr', ops_block, wave_block, preferred_element_type...  38.7 us
    dynamic_update_slice x32, local copies, waits for them, and re-layouts, left_step(): return lax.map(one_sector, (blocks, waves))  28.2 us
  transfers between devices with their start and end apart: 2, of which 2 were waited for; matrix products, arithmetic and copies ran while one was open for 0% of the time, Pallas kernels for 0%

profile of v1, /device:TPU:0, one launch (start us, length us, event | category | flops | bytes accessed | tf_op | source)
XLA Modules:
  0.0 789.7 jit_solution(14845069868140764267)
XLA Ops:
  7.4 1.8 multiply_convert_fusion
  9.1 7.8 tile.4
  16.9 7.2 all-to-all-start
  24.4 292.8 %all-to-all-done = bf16[32,256,4,256]{3,2,1,0:T(4,128)(2,1)} async-done(((bf16[32,256,4,256]{3,2,1,0:T(4,128)(2,1)}), bf16[32,256,4,256]{3,2,1,0:T(4,128)(2,1)}, u32[]{:S(2)}, u32[]{:S(2)}) %all-to-all-start) | async-done | bytes 16777248 | tf_op jit(solution)/shard_map/all_to_all | solution.py:10
  317.2 186.0 %while.10 = (s32[]{:T(128)}, bf16[32,1,256,4,256]{4,2,3,1,0:T(8,128)(2,1)}, bf16[32,1,256,256]{3,2,1,0:T(8,128)(2,1)}, bf16[32,256,4,256]{3,2,1,0:T(4,128)(2,1)}, f32[1,4,4]{2,1,0:T(4,128)S(1)}, /*index=5*/s32[]{:T(128)}) while((s32[]{:T(128)}, bf16[32,1,256,4,256]{4,2,3,1,0:T(8,128)(2,1)}, bf16[32,1,256,256]{3,2,1,0:T(8,128)(2,1)}, ...), condition=%wide.region_1.2_spmd, body=%wide.region_0.1_spmd.sunk | while | flops 147062784 | bytes 5375113 | solution.py:30
  319.6 2.5 fusion.28
  325.4 2.5 fusion.28
  331.2 2.5 fusion.28
  337.1 2.5 fusion.28
  342.9 2.5 fusion.28
  348.7 2.5 fusion.28
  354.5 2.5 fusion.28
  360.3 2.5 fusion.28
  363.7 1.2 dynamic-slice_bitcast_fusion.2
  366.1 2.5 fusion.28
  371.9 2.5 fusion.28
  377.7 2.5 fusion.28
  381.1 1.2 dynamic-slice_bitcast_fusion.2
  383.5 2.5 fusion.28
  386.9 1.2 dynamic-slice_bitcast_fusion.2
  389.4 2.5 fusion.28
  395.2 2.5 fusion.28
  398.6 1.2 dynamic-slice_bitcast_fusion.2
  401.0 2.5 fusion.28
  406.8 2.5 fusion.28
  412.6 2.5 fusion.28
  418.5 2.5 fusion.28
  421.9 1.2 dynamic-slice_bitcast_fusion.2
  424.3 2.5 fusion.28
  430.1 2.5 fusion.28
  433.5 1.2 dynamic-slice_bitcast_fusion.2
  435.9 2.5 fusion.28
  439.3 1.2 dynamic-slice_bitcast_fusion.2
  441.8 2.5 fusion.28
  445.1 1.2 dynamic-slice_bitcast_fusion.2
  447.5 2.5 fusion.28
  453.3 2.5 fusion.28
  459.2 2.5 fusion.28
  465.0 2.5 fusion.28
  470.8 2.5 fusion.28
  476.6 2.5 fusion.28
  482.4 2.5 fusion.28
  488.2 2.5 fusion.28
  494.1 2.5 fusion.28
  499.9 2.5 fusion.28
  503.2 197.7 %all_to_all.23 = bf16[32,1,256,4,256]{4,2,3,1,0:T(8,128)(2,1)} all-to-all(bf16[32,1,256,4,256]{4,2,3,1,0:T(8,128)(2,1)} %get-tuple-element.32), channel_id=1, replica_groups=mesh['op'=16,'sec'=8] {'op'}, dimensions={0} | all-to-all | bytes 33554432 | tf_op jit(solution)/shard_map/all_to_all | solution.py:48
  700.9 9.5 %fusion.12 = f32[2,256,4,256]{3,1,2,0:T(8,128)} fusion(bf16[2,16,1,256,256]{4,3,2,1,0:T(8,128)(2,1)S(1)} %copy-done.2, bf16[16,2,1,256,4,256]{5,3,4,2,1,0:T(8,128)(2,1)} %bitcast.48), kind=kOutput, calls=%fused_computation.16 | convolution fusion | flops 4294967296 | bytes 23068672 | tf_op jit(solution)/shard_map/sklqm,skrm->slqr/dot_general | solution.py:50
  710.5 70.5 %all-reduce.2.cloned.1.call-done = f32[2,256,4,256]{3,1,2,0:T(8,128)} async-done(((f32[2,256,4,256]{3,1,2,0:T(8,128)}), f32[2,256,4,256]{3,1,2,0:T(8,128)}) %all-reduce.2.cloned.1.call-update) | async-done | bytes 2097168 | tf_op jit(solution)/shard_map/psum | solution.py:54
  (104 shorter events, 99.2 us)
Async XLA Ops:
  6.5 17.6 %copy-start = (f32[128,4,4]{0,2,1:T(4,128)S(1)}, f32[128,4,4]{0,2,1:T(4,128)}, u32[]{:S(2)}) copy-start(f32[128,4,4]{0,2,1:T(4,128)} %param.11) | copy-start | bytes 24580
  16.9 300.3 %all-to-all-start = ((bf16[32,256,4,256]{3,2,1,0:T(4,128)(2,1)}), bf16[32,256,4,256]{3,2,1,0:T(4,128)(2,1)}, u32[]{:S(2)}, u32[]{:S(2)}) async-start(bf16[32,256,4,256]{3,2,1,0:T(4,128)(2,1)} %bitcast.47), calls=%async_computation | async-start | bytes 33554432 | tf_op jit(solution)/shard_map/all_to_all | solution.py:10
  24.1 757.0 %all-reduce.2.cloned.1.call-start = ((), (), s32[]{:S(2)}) async-start(), calls=%async_computation.2 | async-start | bytes 4194304 | tf_op jit(solution)/shard_map/psum | solution.py:54
  503.2 197.7 %copy-start.2 = (bf16[2,16,1,256,256]{4,3,2,1,0:T(8,128)(2,1)S(1)}, bf16[2,16,1,256,256]{4,3,2,1,0:T(8,128)(2,1)}, u32[]{:S(2)}) copy-start(bf16[2,16,1,256,256]{4,3,2,1,0:T(8,128)(2,1)} %param.10) | copy-start | bytes 12582916
  700.9 82.0 %copy-start.1 = (f32[128,4,4]{0,2,1:T(4,128)S(1)}, f32[128,4,4]{0,2,1:T(4,128)}, u32[]{:S(2)}) copy-start(f32[128,4,4]{0,2,1:T(4,128)} %param.11) | copy-start | bytes 24580
Sparse Core Ops, SparseCore 0:
  710.6 70.4 all-reduce.1
